TPU v7x, 512 devices: a whole 4x8x8 slice. The times are simulated.
512 devices in a mesh: net: 128 (over z, y, core), scen: 4 (over x).
Axes of the slice: x: 4, y: 8, z: 8, core: 2. Of those that a mesh axis runs over, the one named last changes fastest.
Arguments:
- volt_mag: float32 [30720, 128], P('net', 'scen'), parts along dimension 1, may hold values from 0.94 to 1.06
- volt_ang: float32 [30720, 128], P('net', 'scen'), parts along dimension 1, may hold values from -0.5 to 0.5
- gradient: float32 [30720, 2, 128], P('net', None, 'scen'), parts along dimension 2, may hold values from -40 to 40
- branch_from: int32 [40960], P('net'), may hold values from 0 to 239, as said below
- branch_to: int32 [40960], P('net'), may hold values from 0 to 479, as said below
- branch_count: int32 [128], P('net'), may hold values from 160 to 320, as said below
- boundary: int32 [30720], P('net'), may hold values from 0 to 239, as said below
- conductance: float32 [40960], P('net'), may hold values from 0.2 to 2
- susceptance: float32 [40960], P('net'), may hold values from 1 to 10
- duals: float32 [2, 40960, 128], P(None, 'net', 'scen'), parts along dimension 2, may hold values from 0.02 to 0.2
- slacks: float32 [2, 40960, 128], P(None, 'net', 'scen'), parts along dimension 2, may hold values from 0.2 to 2
- gen_bus: int32 [5120], P('net'), may hold values from 0 to 239
- gen_curvature: float32 [5120], P('net'), may hold values from 1 to 10
Outputs:
- search_step: float32 [30720, 2, 128], P('net', None, 'scen'), parts along dimension 2
- residual: float32 [30720, 2, 128], P('net', None, 'scen'), parts along dimension 2
There are 4 independent parts, one for each index of `scen`. A program takes and returns all parts, laid end to end along the dimension named above; an argument that names none is the same for every part. Nothing has to cross between parts.
Inputs may be any that keep to these rules, and one draw needn't show every extreme that they name: `branch_from`: A bus index within the branch's own device. A branch whose branch_to is 240 + e with e >= 0 starts at boundary entry e of its own device. `branch_to`: below 240: a bus of the same device other than the from-bus. 240 + e for e < 120: entry e of the previous device's list toward this device; 360 + e: entry e of the next device's list toward this device. Only the first 240 slots of a device end at a neighbour, each such value at most once a device; the first device has no ends of the first kind, the last none of the second. `branch_count`: slots at or past a device's count contribute nothing. Some device is full in every draw. `boundary`: per device 2 * 120 distinct local buses: the first 120 face the previous device, the rest the next device.
All inputs are finite; a program needn't handle non-finite values.
Results may differ from a plain program's by a relative error of at most 0.0003.
Values sent between devices are 32-bit elements; how exact they have to be, the bound alone decides.
A program may use at most 64 MiB of HBM per device.

v0:
```python
import jax
import jax.numpy as jnp
from jax import lax
from jax.sharding import PartitionSpec as P

ITERS = 4
barrier_weight = 0.01
volt_low = 0.9
volt_high = 1.1
angle_reg = 0.5


def shifted(array, axis, by):
    peers = lax.axis_size(axis)
    pairs = [(i, i + by) for i in range(peers) if 0 <= i + by < peers]
    return lax.ppermute(array, axis, pairs)


def branch_blocks(
    magnitude_from,
    angle_from,
    magnitude_to,
    angle_to,
    conduct,
    suscept,
    weight_active,
    weight_reactive,
):
    angle_diff = angle_from - angle_to
    cosine_diff = jnp.cos(angle_diff)
    sine_diff = jnp.sin(angle_diff)
    flow_along = conduct * cosine_diff + suscept * sine_diff
    flow_across = conduct * sine_diff - suscept * cosine_diff
    cross_term = magnitude_from * magnitude_to
    active_rows = (
        2.0 * conduct * magnitude_from - magnitude_to * flow_along,
        cross_term * flow_across,
        -magnitude_from * flow_along,
        -cross_term * flow_across,
    )
    reactive_rows = (
        -2.0 * suscept * magnitude_from - magnitude_to * flow_across,
        -cross_term * flow_along,
        -magnitude_from * flow_across,
        cross_term * flow_along,
    )

    def block_entry(left_index, right_index):
        return (
            weight_active * active_rows[left_index] * active_rows[right_index]
            + weight_reactive * reactive_rows[left_index] * reactive_rows[right_index]
        )

    from_block = jnp.stack([block_entry(0, 0), block_entry(0, 1), block_entry(1, 1)], axis=1)
    to_block = jnp.stack([block_entry(2, 2), block_entry(2, 3), block_entry(3, 3)], axis=1)
    cross_block = jnp.stack(
        [block_entry(0, 2), block_entry(0, 3), block_entry(1, 2), block_entry(1, 3)], axis=1
    )
    return (from_block, to_block, cross_block)


def apply_cross(matrix_block, vector):
    return jnp.stack(
        [
            matrix_block[:, 0] * vector[:, 0] + matrix_block[:, 1] * vector[:, 1],
            matrix_block[:, 2] * vector[:, 0] + matrix_block[:, 3] * vector[:, 1],
        ],
        axis=1,
    )


def apply_cross_transposed(matrix_block, vector):
    return jnp.stack(
        [
            matrix_block[:, 0] * vector[:, 0] + matrix_block[:, 2] * vector[:, 1],
            matrix_block[:, 1] * vector[:, 0] + matrix_block[:, 3] * vector[:, 1],
        ],
        axis=1,
    )


def scenario_sum(left_vec, right_vec):
    return jnp.sum(left_vec * right_vec, axis=(0, 1))


def widen(values):
    return values[None, None, :]


def body(
    volt_mag,
    volt_ang,
    gradient,
    branch_from,
    branch_to,
    branch_count,
    boundary,
    conductance,
    susceptance,
    duals,
    slacks,
    gen_bus,
    gen_curvature,
):
    bus_count = volt_mag.shape[0]
    ghost_count = boundary.shape[0] // 2
    extended_size = bus_count + 2 * ghost_count
    slot_count = branch_from.shape[0]
    left_list = boundary[:ghost_count]
    right_list = boundary[ghost_count:]
    left_ghost = slice(bus_count, bus_count + ghost_count)
    right_ghost = slice(bus_count + ghost_count, extended_size)
    return_plan = (
        (-1, left_ghost, right_list, right_ghost),
        (1, right_ghost, left_list, left_ghost),
    )

    def share_vector(values):
        pieces = [values]
        for direction in (1, -1):
            outgoing = jnp.take(values, right_list if direction == 1 else left_list, axis=0)
            pieces.append(shifted(outgoing, "net", direction))
        return jnp.concatenate(pieces, axis=0)

    bus_state = jnp.stack([volt_mag, volt_ang], axis=1)
    pieces = [bus_state]
    for share_direction in (1, -1):
        outgoing = jnp.take(bus_state, right_list if share_direction == 1 else left_list, axis=0)
        pieces.append(shifted(outgoing, "net", share_direction))
    extended_state = jnp.concatenate(pieces, axis=0)
    from_state = jnp.take(extended_state, branch_from, axis=0)
    to_state = jnp.take(extended_state, branch_to, axis=0)
    live_mask = (jnp.arange(slot_count) < branch_count[0]).astype(jnp.float32)[:, None]
    weight_active = live_mask * duals[0] / slacks[0]
    weight_reactive = live_mask * duals[1] / slacks[1]
    from_block, to_block, cross_block = branch_blocks(
        from_state[:, 0],
        from_state[:, 1],
        to_state[:, 0],
        to_state[:, 1],
        conductance[:, None],
        susceptance[:, None],
        weight_active,
        weight_reactive,
    )
    diag_extended = jax.ops.segment_sum(
        from_block, branch_from, num_segments=extended_size
    ) + jax.ops.segment_sum(to_block, branch_to, num_segments=extended_size)
    diag_local = diag_extended[:bus_count]
    for direction, ghost_rows, target_rows, source_rows in return_plan:
        arrived_diag = shifted(diag_extended[ghost_rows], "net", direction)
        diag_local = diag_local.at[target_rows].add(arrived_diag)
    gen_table = (gen_bus[None, :] == jnp.arange(bus_count)[:, None]).astype(jnp.float32)
    gen_sum = jnp.dot(gen_table, gen_curvature, precision=lax.Precision.HIGHEST)[:, None]
    barrier = barrier_weight / jnp.square(volt_mag - volt_low) + barrier_weight / jnp.square(
        volt_high - volt_mag
    )
    diag_vv = diag_local[:, 0] + barrier + gen_sum
    diag_va = diag_local[:, 1]
    diag_aa = diag_local[:, 2] + angle_reg + gen_sum
    determinant = diag_vv * diag_aa - diag_va * diag_va
    inverse_vv = diag_aa / determinant
    inverse_va = -diag_va / determinant
    inverse_aa = diag_vv / determinant

    def precondition(vector):
        return jnp.stack(
            [
                inverse_vv * vector[:, 0] + inverse_va * vector[:, 1],
                inverse_va * vector[:, 0] + inverse_aa * vector[:, 1],
            ],
            axis=1,
        )

    update_field = jnp.zeros_like(gradient)
    residual = gradient

    def energy_of(residual_now, scaled_now):
        return lax.psum(scenario_sum(residual_now, scaled_now), "net")

    scaled = precondition(residual)
    search = scaled
    energy = energy_of(residual, scaled)
    for iteration in range(ITERS):
        extended = share_vector(search)
        from_values = jnp.take(extended, branch_from, axis=0)
        to_values = jnp.take(extended, branch_to, axis=0)
        from_terms = apply_cross(cross_block, to_values)
        to_terms = apply_cross_transposed(cross_block, from_values)
        result = jnp.stack(
            [
                diag_vv * search[:, 0] + diag_va * search[:, 1],
                diag_va * search[:, 0] + diag_aa * search[:, 1],
            ],
            axis=1,
        )
        summed = jax.ops.segment_sum(
            from_terms, branch_from, num_segments=extended_size
        ) + jax.ops.segment_sum(to_terms, branch_to, num_segments=extended_size)
        local_sum = result + summed[:bus_count]
        for apply_direction, apply_ghost_rows, apply_target_rows, apply_source_rows in return_plan:
            arrived = shifted(summed[apply_ghost_rows], "net", apply_direction)
            local_sum = local_sum.at[apply_target_rows].add(arrived)
        step_size = energy / lax.psum(scenario_sum(search, local_sum), "net")
        update_field = update_field + widen(step_size) * search
        residual = residual - widen(step_size) * local_sum
        if iteration + 1 < ITERS:
            scaled = precondition(residual)
            energy_next = energy_of(residual, scaled)
            search = scaled + widen(energy_next / energy) * search
            energy = energy_next
    return (update_field, residual)


def solution(mesh):
    placed = (
        P("net", "scen"),
        P("net", "scen"),
        P("net", None, "scen"),
        P("net"),
        P("net"),
        P("net"),
        P("net"),
        P("net"),
        P("net"),
        P(None, "net", "scen"),
        P(None, "net", "scen"),
        P("net"),
        P("net"),
    )
    return jax.shard_map(
        body,
        mesh=mesh,
        in_specs=placed,
        out_specs=(P("net", None, "scen"), P("net", None, "scen")),
        check_vma=False,
    )
```

profile of v0, /device:TPU:260, one launch (start us, length us, event | category | flops | bytes accessed | tf_op | source)
XLA Modules:
  0.0 2067.8 jit_solution(2405154826822002641)
XLA Ops:
  6.3 7.0 collective-permute-start.1
  15.9 2.0 gather_fusion.2
  18.1 2.0 gather_fusion.3
  22.2 11.9 scatter_fusion.1
  34.3 11.9 scatter_fusion
  46.6 7.1 collective-permute-start.2
  57.4 5.0 scatter_fusion.2
  62.4 2.2 collective-permute-done.3
  64.6 5.0 scatter_fusion.3
  74.6 7.0 collective-permute-start.5
  83.5 2.0 gather_fusion.7
  88.5 11.9 scatter_fusion.5
  100.5 11.9 scatter_fusion.4
  112.9 7.0 collective-permute-start.6
  119.9 2.1 collective-permute-start.7
  122.3 5.0 scatter_fusion.6
  127.3 2.1 collective-permute-done.7
  129.4 5.0 scatter_fusion.7
  134.6 249.9 %all-reduce = (f32[32]{0:T(128)S(1)}, f32[32]{0:T(128)S(1)}) all-reduce(f32[32]{0:T(128)S(1)} %get-tuple-element.11, f32[32]{0:T(128)S(1)} %get-tuple-element.10), channel_id=1, replica_groups=mesh['net'=128,'scen'=4] {'net'}, use_global_device_ids=true, to_apply=%region_5.8 | all-reduce | flops 64 | bytes 512 | tf_op jit(solution)/shard_map/psum | solution.py:179
  384.8 246.8 %psum.58 = f32[32]{0:T(128)S(1)} all-reduce(f32[32]{0:T(128)S(1)} %multiply_reduce_fusion.5), channel_id=1, replica_groups=mesh['net'=128,'scen'=4] {'net'}, use_global_device_ids=true, to_apply=%region_13.16 | all-reduce | flops 32 | bytes 256 | tf_op jit(solution)/shard_map/psum | solution.py:179
  635.4 7.0 collective-permute-start.9
  649.2 11.9 scatter_fusion.9
  661.3 11.9 scatter_fusion.8
  673.7 7.0 collective-permute-start.10
  683.1 5.0 scatter_fusion.10
  688.1 2.1 collective-permute-done.11
  690.2 5.0 scatter_fusion.11
  695.5 249.9 %psum.59 = f32[32]{0:T(128)S(1)} all-reduce(f32[32]{0:T(128)S(1)} %multiply_reduce_fusion.4), channel_id=1, replica_groups=mesh['net'=128,'scen'=4] {'net'}, use_global_device_ids=true, to_apply=%region_19.22 | all-reduce | flops 32 | bytes 256 | tf_op jit(solution)/shard_map/psum | solution.py:204
  945.6 246.8 %psum.60 = f32[32]{0:T(128)S(1)} all-reduce(f32[32]{0:T(128)S(1)} %multiply_reduce_fusion.3), channel_id=1, replica_groups=mesh['net'=128,'scen'=4] {'net'}, use_global_device_ids=true, to_apply=%region_21.24 | all-reduce | flops 32 | bytes 256 | tf_op jit(solution)/shard_map/psum | solution.py:179
  1196.2 7.2 collective-permute-start.13
  1205.1 2.0 gather_fusion.14
  1207.1 2.0 gather_fusion.15
  1210.0 11.9 scatter_fusion.13
  1222.1 11.9 scatter_fusion.12
  1234.5 7.0 collective-permute-start.14
  1243.9 5.0 scatter_fusion.14
  1248.9 2.1 collective-permute-done.15
  1251.0 5.0 scatter_fusion.15
  1256.3 249.9 %psum.61 = f32[32]{0:T(128)S(1)} all-reduce(f32[32]{0:T(128)S(1)} %multiply_reduce_fusion.2), channel_id=1, replica_groups=mesh['net'=128,'scen'=4] {'net'}, use_global_device_ids=true, to_apply=%region_27.30 | all-reduce | flops 32 | bytes 256 | tf_op jit(solution)/shard_map/psum | solution.py:204
  1506.4 246.8 %psum.62 = f32[32]{0:T(128)S(1)} all-reduce(f32[32]{0:T(128)S(1)} %multiply_reduce_fusion.1), channel_id=1, replica_groups=mesh['net'=128,'scen'=4] {'net'}, use_global_device_ids=true, to_apply=%region_29.32 | all-reduce | flops 32 | bytes 256 | tf_op jit(solution)/shard_map/psum | solution.py:179
  1757.1 7.0 collective-permute-start.17
  1770.9 11.9 scatter_fusion.17
  1783.0 11.9 scatter_fusion.16
  1795.3 7.0 collective-permute-start.18
  1804.7 5.0 scatter_fusion.18
  1809.7 2.1 collective-permute-done.19
  1811.8 5.0 scatter_fusion.19
  1817.1 249.9 %psum.63 = f32[32]{0:T(128)S(1)} all-reduce(f32[32]{0:T(128)S(1)} %multiply_reduce_fusion), channel_id=1, replica_groups=mesh['net'=128,'scen'=4] {'net'}, use_global_device_ids=true, to_apply=%region_35.38 | all-reduce | flops 32 | bytes 256 | tf_op jit(solution)/shard_map/psum | solution.py:204
  (230 shorter events, 63.2 us)
Async XLA Ops:
  0.6 55.0 %copy-start = (f32[40]{0:T(128)S(1)}, f32[40]{0:T(128)}, u32[]{:S(2)}) copy-start(f32[40]{0:T(128)} %param.29) | copy-start | bytes 484
  3.4 11.3 collective-permute-start
  6.0 7.2 copy-start.3
  6.3 9.4 collective-permute-start.1
  13.2 0.7 copy-start.4
  13.9 0.7 copy-start.7
  13.9 0.7 copy-start.8
  20.2 0.9 copy-start.5
  20.2 0.9 copy-start.6
  46.6 9.1 copy-start.9
  46.6 10.8 collective-permute-start.2
  53.7 10.8 collective-permute-start.3
  70.0 0.9 copy-start.1
  70.0 0.9 copy-start.2
  72.6 9.0 collective-permute-start.4
  74.6 8.5 collective-permute-start.5
  112.9 9.4 collective-permute-start.6
  119.9 9.5 collective-permute-start.7
  633.4 9.0 collective-permute-start.8
  635.4 8.5 collective-permute-start.9
  673.7 9.4 collective-permute-start.10
  680.7 9.5 collective-permute-start.11
  1194.2 9.2 collective-permute-start.12
  1196.2 8.5 collective-permute-start.13
  1234.5 9.4 collective-permute-start.14
  1241.5 9.5 collective-permute-start.15
  1755.1 9.0 collective-permute-start.16
  1757.1 8.5 collective-permute-start.17
  1795.3 9.4 collective-permute-start.18
  1802.3 9.5 collective-permute-start.19
where the time goes:
time: 2070 us
  blocking collectives  1740 us (84%)
  other arithmetic  177 us (9%)
  starting transfers between devices  89.4 us (4%)
  local copies, waits for them, and re-layouts  38.9 us (2%)
    psum x4, blocking collectives, energy_of(): return lax.psum(scenario_sum(residual_now, scaled_now), 'net')  990 us
    psum x3, blocking collectives, body(): step_size = energy / lax.psum(scenario_sum(search, local_sum), 'net')  750 us
    ppermute x20, starting transfers between devices, shifted(): return lax.ppermute(array, axis, pairs)  89.4 us
    scatter-add x4, other arithmetic, body(): jax.ops.segment_sum(to_terms, branch_to, num_segments=extended_size)  47.8 us
    scatter-add x4, other arithmetic, body(): jax.ops.segment_sum(from_terms, branch_from, num_segments=extended_size)  47.8 us
  transfers between devices with their start and end apart: 20, of which 15 were waited for; matrix products, arithmetic and copies ran while one was open for 1% of the time, Pallas kernels for 0%

commit v1 on v0

--- a/solution.py
+++ b/solution.py
@@ -201,7 +201,7 @@
         for apply_direction, apply_ghost_rows, apply_target_rows, apply_source_rows in return_plan:
             arrived = shifted(summed[apply_ghost_rows], "net", apply_direction)
             local_sum = local_sum.at[apply_target_rows].add(arrived)
-        step_size = energy / lax.psum(scenario_sum(search, local_sum), "net")
+        step_size = energy / jnp.sum(lax.all_gather(scenario_sum(search, local_sum), "net"), axis=0)
         update_field = update_field + widen(step_size) * search
         residual = residual - widen(step_size) * local_sum
         if iteration + 1 < ITERS:

time: 2070 us -> 3050 us (1.47)
  blocking collectives: 1740 us -> 2720 us
    unnamed x0 -> x3, blocking collectives: none -> 1480 us
    psum x3 -> x0, blocking collectives: 750 us -> none  [body(): step_size = energy / lax.psum(scenario_sum(search, local_sum), 'net')]
    psum x4, blocking collectives: 990 us -> 1230 us  [energy_of(): return lax.psum(scenario_sum(residual_now, scaled_now), 'net')]
  transfers between devices with their start and end apart: 20 -> 20, of which waited for: 15 -> 14; matrix products, arithmetic and copies ran while one was open for 1% -> 1% of each run, Pallas kernels for 0% -> 0%
where the time goes in v1:
time: 3050 us
  blocking collectives  2720 us (89%)
  other arithmetic  177 us (6%)
  starting transfers between devices  89.4 us (3%)
  local copies, waits for them, and re-layouts  41.6 us (1%)
    unnamed x3, blocking collectives  1480 us
    psum x4, blocking collectives, energy_of(): return lax.psum(scenario_sum(residual_now, scaled_now), 'net')  1230 us
    ppermute x20, starting transfers between devices, shifted(): return lax.ppermute(array, axis, pairs)  89.4 us
  transfers between devices with their start and end apart: 20, of which 14 were waited for; matrix products, arithmetic and copies ran while one was open for 1% of the time, Pallas kernels for 0%

profile of v1, /device:TPU:260, one launch (start us, length us, event | category | flops | bytes accessed | tf_op | source)
XLA Modules:
  0.0 3045.8 jit_solution(12829640220455126163)
XLA Ops:
  6.3 7.0 collective-permute-start.1
  15.9 2.0 gather_fusion.2
  18.1 2.0 gather_fusion.3
  22.2 11.9 scatter_fusion.1
  34.3 11.9 scatter_fusion
  46.6 7.1 collective-permute-start.2
  58.0 5.0 scatter_fusion.2
  64.6 5.0 scatter_fusion.3
  74.6 7.0 collective-permute-start.5
  85.5 2.0 gather_fusion.6
  88.5 11.9 scatter_fusion.5
  100.5 11.9 scatter_fusion.4
  112.9 7.0 collective-permute-start.6
  119.9 2.1 collective-permute-start.7
  122.3 5.0 scatter_fusion.6
  127.3 2.3 collective-permute-done.7
  129.6 5.0 scatter_fusion.7
  135.1 493.8 %all-reduce.4 = (f32[32]{0:T(128)S(1)}, f32[4096]{0:T(1024)S(1)}) all-reduce(f32[32]{0:T(128)S(1)} %get-tuple-element.11, f32[4096]{0:T(1024)S(1)} %dynamic-update-slice), channel_id=1, replica_groups=mesh['net'=128,'scen'=4] {'net'}, use_global_device_ids=true, to_apply=%region_5.8 | all-reduce | flops 4128 | bytes 33024 | tf_op jit(solution)/shard_map/psum | solution.py:179
  629.3 246.8 %psum.29 = f32[32]{0:T(128)S(1)} all-reduce(f32[32]{0:T(128)S(1)} %multiply_reduce_fusion.5), channel_id=1, replica_groups=mesh['net'=128,'scen'=4] {'net'}, use_global_device_ids=true, to_apply=%region_13.16 | all-reduce | flops 32 | bytes 256 | tf_op jit(solution)/shard_map/psum | solution.py:179
  879.9 7.0 collective-permute-start.9
  888.8 2.0 gather_fusion.10
  893.7 11.9 scatter_fusion.9
  905.8 11.9 scatter_fusion.8
  918.2 7.0 collective-permute-start.10
  927.6 5.0 scatter_fusion.10
  932.6 2.1 collective-permute-done.11
  934.7 5.0 scatter_fusion.11
  940.3 494.0 %all-reduce.1 = f32[4096]{0:T(1024)S(1)} all-reduce(f32[4096]{0:T(1024)S(1)} %dynamic-update-slice.1), channel_id=3, replica_groups=mesh['net'=128,'scen'=4] {'net'}, use_global_device_ids=true, to_apply=%add.1 | all-reduce | flops 4096 | bytes 32768
  1434.6 246.8 %psum.30 = f32[32]{0:T(128)S(1)} all-reduce(f32[32]{0:T(128)S(1)} %multiply_reduce_fusion.3), channel_id=1, replica_groups=mesh['net'=128,'scen'=4] {'net'}, use_global_device_ids=true, to_apply=%region_21.24 | all-reduce | flops 32 | bytes 256 | tf_op jit(solution)/shard_map/psum | solution.py:179
  1685.3 7.2 collective-permute-start.13
  1694.1 2.0 gather_fusion.14
  1696.1 2.0 gather_fusion.15
  1699.0 11.9 scatter_fusion.13
  1711.1 11.9 scatter_fusion.12
  1723.5 7.0 collective-permute-start.14
  1732.9 5.0 scatter_fusion.14
  1737.9 2.1 collective-permute-done.15
  1740.0 5.0 scatter_fusion.15
  1745.6 494.0 %all-reduce.2 = f32[4096]{0:T(1024)S(1)} all-reduce(f32[4096]{0:T(1024)S(1)} %dynamic-update-slice.2), channel_id=4, replica_groups=mesh['net'=128,'scen'=4] {'net'}, use_global_device_ids=true, to_apply=%add.2 | all-reduce | flops 4096 | bytes 32768
  2239.9 246.8 %psum.31 = f32[32]{0:T(128)S(1)} all-reduce(f32[32]{0:T(128)S(1)} %multiply_reduce_fusion.1), channel_id=1, replica_groups=mesh['net'=128,'scen'=4] {'net'}, use_global_device_ids=true, to_apply=%region_29.32 | all-reduce | flops 32 | bytes 256 | tf_op jit(solution)/shard_map/psum | solution.py:179
  2490.6 7.0 collective-permute-start.17
  2504.4 11.9 scatter_fusion.17
  2516.5 11.9 scatter_fusion.16
  2528.8 7.0 collective-permute-start.18
  2538.2 5.0 scatter_fusion.18
  2543.2 2.1 collective-permute-done.19
  2545.3 5.0 scatter_fusion.19
  2550.9 494.0 %all-reduce.3 = f32[4096]{0:T(1024)S(1)} all-reduce(f32[4096]{0:T(1024)S(1)} %dynamic-update-slice.3), channel_id=5, replica_groups=mesh['net'=128,'scen'=4] {'net'}, use_global_device_ids=true, to_apply=%add.3 | all-reduce | flops 4096 | bytes 32768
  (247 shorter events, 64.3 us)
Async XLA Ops:
  0.6 55.0 %copy-start = (f32[40]{0:T(128)S(1)}, f32[40]{0:T(128)}, u32[]{:S(2)}) copy-start(f32[40]{0:T(128)} %param.29) | copy-start | bytes 484
  3.4 11.3 collective-permute-start
  6.0 7.2 copy-start.3
  6.3 9.4 collective-permute-start.1
  13.2 0.7 copy-start.4
  13.9 0.7 copy-start.7
  13.9 0.7 copy-start.8
  20.2 0.9 copy-start.5
  20.2 0.9 copy-start.6
  46.6 9.1 copy-start.9
  46.6 11.3 collective-permute-start.2
  53.7 10.8 collective-permute-start.3
  70.0 0.9 copy-start.1
  70.0 0.9 copy-start.2
  72.6 9.0 collective-permute-start.4
  74.6 8.5 collective-permute-start.5
  112.9 9.4 collective-permute-start.6
  119.9 9.7 collective-permute-start.7
  877.9 9.0 collective-permute-start.8
  879.9 8.5 collective-permute-start.9
  918.2 9.4 collective-permute-start.10
  925.2 9.5 collective-permute-start.11
  1683.2 9.2 collective-permute-start.12
  1685.3 8.5 collective-permute-start.13
  1723.5 9.4 collective-permute-start.14
  1730.5 9.5 collective-permute-start.15
  2488.6 9.0 collective-permute-start.16
  2490.6 8.5 collective-permute-start.17
  2528.8 9.4 collective-permute-start.18
  2535.8 9.5 collective-permute-start.19
